TPU v7x, 32 devices: a whole 2x2x4 slice. The times are simulated.
32 devices in a mesh: gx: 8 (over y, x, core), gy: 4 (over z).
Axes of the slice: x: 2, y: 2, z: 4, core: 2. Of those that a mesh axis runs over, the one named last changes fastest.
Arguments:
- velocity: float32 [3, 1, 384, 1024], P(None, None, 'gy', 'gx'), may hold values from -6 to 6
- block_inverse: float32 [384, 96], P('gy'), may hold values from -1.6 to 1.6, as said below
- lower_map: float32 [384, 96], P('gy'), may hold values from -1 to 1
- upper_map: float32 [384, 96], P('gy'), may hold values from -1 to 1
Outputs:
- new_velocity: float32 [3, 1, 384, 2048], P(None, None, 'gy', 'gx')
Inputs may be any that keep to these rules, and one draw needn't show every extreme that they name: `block_inverse`: entries of the given block inverses.
All inputs are finite; a program needn't handle non-finite values.
Results may differ from a plain program's by a relative error of at most 0.00012.
Values sent between devices are 32-bit elements; how exact they have to be, the bound alone decides.
A program may use at most 64 MiB of HBM per device.

v0:
```python
import math
import jax
import jax.numpy as jnp
from jax import lax
from jax.sharding import PartitionSpec as P

courant = 0.8


def from_partner(shard, axis, bit):
    return lax.ppermute(shard, axis, [(i, i ^ 1 << bit) for i in range(lax.axis_size(axis))])


def reversed_position(position, levels):
    result = jnp.zeros((), jnp.int32)
    for digit_place in range(levels):
        result = result + (position >> digit_place & 1) * (1 << levels - 1 - digit_place)
    return result


def advance(matrix, state):
    return jnp.einsum("ab,spbw->spaw", matrix, state, precision=lax.Precision.HIGHEST)


def local_transform(paired, leading, count_gx, total_x):
    local_x = paired.shape[-1] // 2
    cells = jnp.arange(local_x, dtype=jnp.int32)
    wavenumbers = leading + count_gx * cells
    phases = cells[:, None] * wavenumbers[None, :] % total_x
    angles = 2.0 * math.pi / total_x * phases.astype(jnp.float32)
    cosine = jnp.cos(angles)
    sine_table = jnp.sin(angles)
    transform_matrix = jnp.concatenate(
        [jnp.concatenate([cosine, -sine_table], 1), jnp.concatenate([sine_table, cosine], 1)], 0
    )
    product = jnp.dot(
        paired,
        transform_matrix,
        precision=lax.Precision.HIGHEST,
        preferred_element_type=jnp.float32,
    )
    return product * (1.0 / math.sqrt(total_x))


def local_sweeps(lower_blocks, upper_blocks, loads):

    def step_once(state_prev, inputs):
        fresh = inputs[1] + advance(inputs[0], state_prev)
        return (fresh, fresh)

    start_state = jnp.zeros(loads.shape[1:], jnp.float32)
    unused, sweeps = lax.scan(step_once, start_state, (lower_blocks, loads))
    unused, solved = lax.scan(step_once, start_state, (upper_blocks, sweeps), reverse=True)
    return solved


def shards(velocity, block_inverse, lower_map, upper_map):
    fluxes = velocity[0:1] * velocity
    fields = jnp.concatenate([velocity, fluxes], 0)
    planes_here = fields.shape[1]
    rows_here = fields.shape[2]
    local_x = fields.shape[3]
    count_gx = lax.axis_size("gx")
    levels = count_gx.bit_length() - 1
    position = lax.axis_index("gx")
    total_x = local_x * count_gx
    current = jnp.stack([fields, jnp.zeros_like(fields)])
    for digit_place in reversed(range(levels)):
        half_span = 1 << digit_place
        if digit_place == levels - 1:
            real_partner = from_partner(fields, "gx", digit_place)
            partner = jnp.stack([real_partner, jnp.zeros_like(real_partner)])
        else:
            partner = from_partner(current, "gx", digit_place)
        is_upper = position >> digit_place & 1 == 1
        offset = (position & half_span - 1).astype(jnp.float32)
        angles = offset * (-math.pi / half_span)
        cosine = jnp.cos(angles)
        sine_value = jnp.sin(angles)
        diff_real = partner[0] - current[0]
        diff_imag = partner[1] - current[1]
        turned = jnp.stack(
            [
                diff_real * cosine - diff_imag * sine_value,
                diff_real * sine_value + diff_imag * cosine,
            ]
        )
        current = jnp.where(is_upper, turned, current + partner)
    paired = jnp.concatenate([current[0], current[1]], -1)
    leading = reversed_position(position, levels)
    spectra = local_transform(paired, leading, count_gx, total_x)
    velocity_modes = spectra[:3]
    flux_modes = spectra[3:]
    wavenumbers = leading + count_gx * jnp.arange(local_x, dtype=jnp.int32)
    signed = jnp.where(wavenumbers < total_x // 2, wavenumbers, wavenumbers - total_x)
    factor = courant * signed.astype(jnp.float32) / (total_x // 2)
    side_real = velocity_modes[..., :local_x] + factor * flux_modes[..., local_x:]
    side_imag = velocity_modes[..., local_x:] - factor * flux_modes[..., :local_x]
    right_side = jnp.concatenate([side_real, side_imag], -1)
    loads = advance(block_inverse, right_side)
    count_gy = lax.axis_size("gy")
    column_total = loads.shape[-1]
    column_count = column_total // count_gy
    lowers, uppers = (
        lax.all_gather(lower_map, "gy", axis=0, tiled=True),
        lax.all_gather(upper_map, "gy", axis=0, tiled=True),
    )
    lower_blocks = lowers.reshape(count_gy, rows_here, rows_here)
    upper_blocks = uppers.reshape(count_gy, rows_here, rows_here)
    grouped = loads.reshape(3, planes_here, rows_here, count_gy, column_count)
    profiles = lax.all_to_all(grouped, "gy", split_axis=3, concat_axis=2, tiled=True)
    items = profiles.shape[0]
    blocked = profiles.reshape(items, planes_here, count_gy, rows_here, column_count)
    blocked = jnp.moveaxis(blocked, 2, 0)
    solved_blocks = local_sweeps(lower_blocks, upper_blocks, blocked)
    whole = jnp.moveaxis(solved_blocks, 0, 2).reshape(
        items, planes_here, count_gy * rows_here, 1, column_count
    )
    finished = lax.all_to_all(whole, "gy", split_axis=2, concat_axis=3, tiled=True)
    solved = finished.reshape(3, planes_here, rows_here, column_total)
    return solved


def solution(mesh):
    return jax.shard_map(
        shards,
        mesh=mesh,
        in_specs=(P(None, None, "gy", "gx"), P("gy", None), P("gy", None), P("gy", None)),
        out_specs=P(None, None, "gy", "gx"),
        check_vma=False,
    )
```

profile of v0, /device:TPU:0, one launch (start us, length us, event | category | flops | bytes accessed | tf_op | source)
XLA Modules:
  0.0 91.6 jit_solution(16802690939830432598)
XLA Ops:
  0.0 0.0 copy-start
  0.0 0.8 slice_bitcast_fusion.2
  0.8 1.0 %broadcast_multiply_fusion = f32[3,1,96,128]{3,2,0,1:T(8,128)S(1)} fusion(f32[96,128]{1,0:T(8,128)S(1)} %slice_bitcast_fusion.2, f32[3,1,96,128]{3,2,1,0:T(8,128)} %param.8), kind=kLoop, calls=%fused_computation.53 | loop fusion | flops 36864 | bytes 344064 | tf_op jit(solution)/shard_map/mul | solution.py:58
  1.8 0.0 copy-done.1
  1.9 3.1 %collective-permute-start = (f32[6,1,96,128]{3,2,0,1:T(8,128)S(1)}, f32[6,1,96,128]{3,2,0,1:T(8,128)S(1)}, u32[]{:S(2)}, u32[]{:S(2)}) collective-permute-start(f32[6,1,96,128]{3,2,0,1:T(8,128)S(1)} %pad_maximum_fusion), channel_id=1, source_target_pairs={{0,16},{4,20},{8,24},{12,28},{16,0},{20,4},{24,8},{28,12},{1,17},{... | collective-permute-start | bytes 884744 | tf_op jit(solution)/shard_map/ppermute | solution.py:11
  5.1 6.8 %collective-permute-done = f32[6,1,96,128]{3,2,0,1:T(8,128)S(1)} collective-permute-done((f32[6,1,96,128]{3,2,0,1:T(8,128)S(1)}, f32[6,1,96,128]{3,2,0,1:T(8,128)S(1)}, u32[]{:S(2)}, u32[]{:S(2)}) %collective-permute-start) | collective-permute-done | bytes 294944 | tf_op jit(solution)/shard_map/ppermute | solution.py:11
  11.9 0.1 subtract_bitcast_fusion
  12.0 0.1 maximum_select_fusion
  12.1 1.8 %collective-permute-start.1 = (f32[2,6,1,96,128]{4,3,1,2,0:T(8,128)S(1)}, f32[2,6,1,96,128]{4,3,1,2,0:T(8,128)S(1)}, u32[]{:S(2)}, u32[]{:S(2)}) collective-permute-start(f32[2,6,1,96,128]{4,3,1,2,0:T(8,128)S(1)} %maximum_select_fusion), channel_id=1, source_target_pairs={{0,8},{4,12},{8,0},{12,4},{16,24},{20,28},{24,16},{28,20},{1,9},{5... | collective-permute-start | bytes 1769480 | tf_op jit(solution)/shard_map/ppermute | solution.py:11
  14.0 12.6 %collective-permute-done.1 = f32[2,6,1,96,128]{4,3,1,2,0:T(8,128)S(1)} collective-permute-done((f32[2,6,1,96,128]{4,3,1,2,0:T(8,128)S(1)}, f32[2,6,1,96,128]{4,3,1,2,0:T(8,128)S(1)}, u32[]{:S(2)}, u32[]{:S(2)}) %collective-permute-start.1) | collective-permute-done | bytes 589856 | tf_op jit(solution)/shard_map/ppermute | solution.py:11
  26.6 0.1 multiply_subtract_fusion.1
  26.7 0.1 maximum_select_fusion.1
  26.9 0.1 collective-permute-start.2
  27.0 0.3 fusion.30
  27.3 1.7 %collective-permute-done.2 = f32[2,6,1,96,128]{4,3,1,2,0:T(8,128)S(1)} collective-permute-done((f32[2,6,1,96,128]{4,3,1,2,0:T(8,128)S(1)}, f32[2,6,1,96,128]{4,3,1,2,0:T(8,128)S(1)}, u32[]{:S(2)}, u32[]{:S(2)}) %collective-permute-start.2) | collective-permute-done | bytes 589856 | tf_op jit(solution)/shard_map/ppermute | solution.py:11
  29.0 0.1 multiply_subtract_fusion
  29.0 0.1 maximum_select_fusion.2
  29.2 0.6 fusion.8
  29.9 0.4 convolution_bitcast_fusion
  30.3 0.2 copy.27
  30.5 0.8 copy.28
  31.2 4.9 %all-to-all-start = ((f32[3,1,96,4,64]{2,4,0,1,3:T(8,128)}), f32[3,1,96,4,64]{2,4,0,1,3:T(8,128)S(1)}, u32[]{:S(2)}, u32[]{:S(2)}) async-start(f32[3,1,96,4,64]{2,4,0,1,3:T(8,128)} %copy.28), calls=%async_computation | async-start | bytes 786432 | tf_op jit(solution)/shard_map/all_to_all | solution.py:111
  36.2 0.0 copy-done.2
  36.2 19.4 %all_gather.6 = f32[384,96]{1,0:T(8,128)S(1)} all-gather(f32[96,96]{1,0:T(8,128)S(1)} %copy-done.2), channel_id=1, replica_groups=mesh['gx'=8,'gy'=4] {'gy'}, dimensions={0}, use_global_device_ids=true | all-gather | bytes 184320 | tf_op jit(solution)/shard_map/all_gather | solution.py:105
  55.6 0.0 copy-done.3
  55.6 13.6 %all_gather.7 = f32[384,96]{1,0:T(8,128)S(1)} all-gather(f32[96,96]{1,0:T(8,128)S(1)} %copy-done.3), channel_id=1, replica_groups=mesh['gx'=8,'gy'=4] {'gy'}, dimensions={0}, use_global_device_ids=true | all-gather | bytes 184320 | tf_op jit(solution)/shard_map/all_gather | solution.py:106
  69.2 0.0 all-to-all-done
  69.2 1.3 %while.30 = (s32[]{:T(128)}, f32[3,1,96,64]{2,3,0,1:T(8,128)S(1)}, f32[4,3,1,96,64]{3,4,1,2,0:T(8,128)S(1)}, f32[4,3,1,96,64]{3,4,1,2,0:T(8,128)S(1)}, f32[4,96,96]{2,1,0:T(8,128)S(1)}, /*index=5*/s32[]{:T(128)}, s32[]{:T(128)}) while((s32[]{:T(128)}, f32[3,1,96,64]{2,3,0,1:T(8,128)S(1)}, f32[4,3,1,96,64]{3,4,1,2,0:T(8,128)S(1)}, ...), condition=%wide.region_1.2_spmd.clone, body=%wide.region_0.1_spmd.clone.sunk | while | flops 21270532 | bytes 786527 | solution.py:52
  69.3 0.2 fusion.46
  69.6 0.3 fusion.46
  69.9 0.3 fusion.46
  70.2 0.3 fusion.46
  70.6 1.3 %while.31 = (s32[]{:T(128)}, f32[3,1,96,64]{2,3,0,1:T(8,128)S(1)}, f32[4,3,1,96,64]{3,4,1,2,0:T(8,128)S(1)}, f32[4,3,1,96,64]{3,4,1,2,0:T(8,128)S(1)}, f32[4,96,...) while((s32[]{:T(128)}, f32[3,1,96,64]{2,3,0,1:T(8,128)S(1)}, ...), condition=%wide.region_3.4_spmd.clone, body=%wide.region_2.3_spmd.clone.sunk | while | flops 21270532 | bytes 786547 | solution.py:53
  70.6 0.2 fusion.49
  70.9 0.3 fusion.49
  71.3 0.2 fusion.49
  71.6 0.3 fusion.49
  71.9 0.3 copy.35
  72.2 0.7 reshape.122
  73.0 0.5 broadcast.111
  73.5 2.6 %reduce = f32[384,3,64]{2,1,0:T(4,128)S(1)} reduce(f32[384,3,1,1,64]{4,3,2,1,0:T(1,128)S(1)} %bitcast.125, f32[]{:T(128)} %broadcast.111), dimensions={2,3}, to_apply=%bitcast.93.reduce_sub_computation | reduce | bytes 589828
  76.1 0.6 reshape.123
  76.7 10.8 %all_to_all.30 = f32[4,1,18432]{2,1,0:T(1,128)S(1)} all-to-all(f32[4,1,18432]{2,1,0:T(1,128)S(1)} %reshape.123), channel_id=1, replica_groups=mesh['gx'=8,'gy'=4] {'gy'}, dimensions={0} | all-to-all | bytes 589824 | tf_op jit(solution)/shard_map/all_to_all | solution.py:119
  87.5 1.5 %reduce.1 = f32[4,18432]{1,0:T(4,128)S(1)} reduce(f32[4,1,18432]{2,1,0:T(1,128)S(1)} %all_to_all.30, f32[]{:T(128)} %broadcast.111), dimensions={1}, to_apply=%all_to_all.25.reduce_sub_computation | reduce | bytes 589828 | tf_op jit(solution)/shard_map/all_to_all | solution.py:119
  88.9 0.7 reshape.124
  89.7 0.8 copy.32
  90.5 0.3 all_to_all.26
  90.8 0.9 copy.34
  (30 shorter events, 0.5 us)
Async XLA Ops:
  0.0 29.9 %copy-start = (f32[96,96]{1,0:T(8,128)S(1)}, f32[96,96]{1,0:T(8,128)}, u32[]{:S(2)}) copy-start(f32[96,96]{1,0:T(8,128)} %param.9) | copy-start | bytes 110596
  0.8 1.0 %copy-start.1 = (f32[3,1,96,128]{3,2,1,0:T(8,128)S(1)}, f32[3,1,96,128]{3,2,1,0:T(8,128)}, u32[]{:S(2)}) copy-start(f32[3,1,96,128]{3,2,1,0:T(8,128)} %param.8) | copy-start | bytes 442372
  1.9 10.1 %collective-permute-start = (f32[6,1,96,128]{3,2,0,1:T(8,128)S(1)}, f32[6,1,96,128]{3,2,0,1:T(8,128)S(1)}, u32[]{:S(2)}, u32[]{:S(2)}) collective-permute-start(f32[6,1,96,128]{3,2,0,1:T(8,128)S(1)} %pad_maximum_fusion), channel_id=1, source_target_pairs={{0,16},{4,20},{8,24},{12,28},{16,0},{20,4},{24,8},{28,12},{1,17},{... | collective-permute-start | bytes 884744 | tf_op jit(solution)/shard_map/ppermute | solution.py:11
  12.1 14.6 %collective-permute-start.1 = (f32[2,6,1,96,128]{4,3,1,2,0:T(8,128)S(1)}, f32[2,6,1,96,128]{4,3,1,2,0:T(8,128)S(1)}, u32[]{:S(2)}, u32[]{:S(2)}) collective-permute-start(f32[2,6,1,96,128]{4,3,1,2,0:T(8,128)S(1)} %maximum_select_fusion), channel_id=1, source_target_pairs={{0,8},{4,12},{8,0},{12,4},{16,24},{20,28},{24,16},{28,20},{1,9},{5... | collective-permute-start | bytes 1769480 | tf_op jit(solution)/shard_map/ppermute | solution.py:11
  26.9 2.1 %collective-permute-start.2 = (f32[2,6,1,96,128]{4,3,1,2,0:T(8,128)S(1)}, f32[2,6,1,96,128]{4,3,1,2,0:T(8,128)S(1)}, u32[]{:S(2)}, u32[]{:S(2)}) collective-permute-start(f32[2,6,1,96,128]{4,3,1,2,0:T(8,128)S(1)} %maximum_select_fusion.1), channel_id=1, source_target_pairs={{0,4},{4,0},{8,12},{12,8},{16,20},{20,16},{24,28},{28,24},{1,5},{5... | collective-permute-start | bytes 1769480 | tf_op jit(solution)/shard_map/ppermute | solution.py:11
  31.2 4.9 %copy-start.2 = (f32[96,96]{1,0:T(8,128)S(1)}, f32[96,96]{1,0:T(8,128)}, u32[]{:S(2)}) copy-start(f32[96,96]{1,0:T(8,128)} %param.10) | copy-start | bytes 110596
  31.2 37.9 %all-to-all-start = ((f32[3,1,96,4,64]{2,4,0,1,3:T(8,128)}), f32[3,1,96,4,64]{2,4,0,1,3:T(8,128)S(1)}, u32[]{:S(2)}, u32[]{:S(2)}) async-start(f32[3,1,96,4,64]{2,4,0,1,3:T(8,128)} %copy.28), calls=%async_computation | async-start | bytes 786432 | tf_op jit(solution)/shard_map/all_to_all | solution.py:111
  36.2 19.4 %copy-start.3 = (f32[96,96]{1,0:T(8,128)S(1)}, f32[96,96]{1,0:T(8,128)}, u32[]{:S(2)}) copy-start(f32[96,96]{1,0:T(8,128)} %param.11) | copy-start | bytes 110596
where the time goes:
time: 92 us; the launch traced here: 91.6 us
  blocking collectives  43.8 us (48%)
  waiting for transfers between devices  21.1 us (23%)
  starting transfers between devices  9.85 us (11%)
  local copies, waits for them, and re-layouts  6.69 us (7%)
  other arithmetic  6.21 us (7%)
  matrix products  3.06 us (3%)
    ppermute x3, waiting for transfers between devices, from_partner(): lax.ppermute(shard, axis, [(i, i ^ 1 << bit) for i in range(lax.axis_size...  21.1 us
    all_gather x1, blocking collectives, shards(): lax.all_gather(lower_map, 'gy', axis=0, tiled=True)  19.4 us
    all_gather x1, blocking collectives, shards(): lax.all_gather(upper_map, 'gy', axis=0, tiled=True)  13.6 us
    all_to_all x1, blocking collectives, shards(): lax.all_to_all(whole, 'gy', split_axis=2, concat_axis=3, tiled=True)  10.8 us
    all_to_all x1, starting transfers between devices, shards(): lax.all_to_all(grouped, 'gy', split_axis=3, concat_axis=2, tiled=True)  4.94 us
    ppermute x3, starting transfers between devices, from_partner(): lax.ppermute(shard, axis, [(i, i ^ 1 << bit) for i in range(lax.axis_size...  4.91 us
    unnamed x3, other arithmetic  2.57 us
    while x8, matrix products  2.02 us
  transfers between devices with their start and end apart: 4, of which 3 were waited for; matrix products, arithmetic and copies ran while one was open for 0% of the time, Pallas kernels for 0%

commit v1 on v0

--- a/solution.py
+++ b/solution.py
@@ -5,6 +5,18 @@
 from jax.sharding import PartitionSpec as P
 
 courant = 0.8
+
+
+def sent_to_each(value, axis, split, join):
+    ways, here = (lax.axis_size(axis), lax.axis_index(axis))
+    width = value.shape[split] // ways
+    turned = jnp.roll(value, -here * width, axis=split)
+    got = [lax.slice_in_dim(turned, 0, width, axis=split)]
+    for far in range(1, ways):
+        sent = lax.slice_in_dim(turned, far * width, (far + 1) * width, axis=split)
+        got.append(lax.ppermute(sent, axis, [(d, (d + far) % ways) for d in range(ways)]))
+    line = jnp.concatenate(got[::-1], axis=join)
+    return jnp.roll(line, (here + 1) * got[0].shape[join], axis=join)
 
 
 def from_partner(shard, axis, bit):
@@ -108,7 +120,7 @@
     lower_blocks = lowers.reshape(count_gy, rows_here, rows_here)
     upper_blocks = uppers.reshape(count_gy, rows_here, rows_here)
     grouped = loads.reshape(3, planes_here, rows_here, count_gy, column_count)
-    profiles = lax.all_to_all(grouped, "gy", split_axis=3, concat_axis=2, tiled=True)
+    profiles = sent_to_each(grouped, "gy", 3, 2)
     items = profiles.shape[0]
     blocked = profiles.reshape(items, planes_here, count_gy, rows_here, column_count)
     blocked = jnp.moveaxis(blocked, 2, 0)

time: 92 us -> 89.1 us (0.968)
  blocking collectives: 43.8 us -> 40.8 us
    all_to_all x1 -> x0, starting transfers between devices: 4.94 us -> none  [shards(): lax.all_to_all(grouped, 'gy', split_axis=3, concat_axis=2, tiled=True)]
    ppermute x0 -> x3, starting transfers between devices: none -> 4.61 us  [sent_to_each(): lax.ppermute(sent, axis, [(d, (d + far) % ways) for d in range(ways)])]
    all_gather x1, blocking collectives: 19.4 us -> 16.9 us  [shards(): lax.all_gather(lower_map, 'gy', axis=0, tiled=True)]
  transfers between devices with their start and end apart: 4 -> 6, of which waited for: 3 -> 3; matrix products, arithmetic and copies ran while one was open for 0% -> 0% of each run, Pallas kernels for 0% -> 0%
where the time goes in v1:
time: 89.1 us; the launch traced here: 88.8 us
  blocking collectives  40.8 us (46%)
  waiting for transfers between devices  21.1 us (24%)
  starting transfers between devices  9.52 us (11%)
  local copies, waits for them, and re-layouts  7.02 us (8%)
  other arithmetic  6.28 us (7%)
  matrix products  3.07 us (3%)
    ppermute x3, waiting for transfers between devices, from_partner(): lax.ppermute(shard, axis, [(i, i ^ 1 << bit) for i in range(lax.axis_size...  21.1 us
    all_gather x1, blocking collectives, shards(): lax.all_gather(lower_map, 'gy', axis=0, tiled=True)  16.9 us
    all_gather x1, blocking collectives, shards(): lax.all_gather(upper_map, 'gy', axis=0, tiled=True)  13.6 us
    all_to_all x1, blocking collectives, shards(): lax.all_to_all(whole, 'gy', split_axis=2, concat_axis=3, tiled=True)  10.3 us
    ppermute x3, starting transfers between devices, from_partner(): lax.ppermute(shard, axis, [(i, i ^ 1 << bit) for i in range(lax.axis_size...  4.91 us
    ppermute x3, starting transfers between devices, sent_to_each(): lax.ppermute(sent, axis, [(d, (d + far) % ways) for d in range(ways)])  4.61 us
    unnamed x3, other arithmetic  2.57 us
    while x8, matrix products  2.02 us
  transfers between devices with their start and end apart: 6, of which 3 were waited for; matrix products, arithmetic and copies ran while one was open for 0% of the time, Pallas kernels for 0%

profile of v1, /device:TPU:0, one launch (start us, length us, event | category | flops | bytes accessed | tf_op | source)
XLA Modules:
  0.0 88.8 jit_solution(3186775546613749043)
XLA Ops:
  0.0 0.8 slice_bitcast_fusion.2
  0.8 1.0 %broadcast_multiply_fusion = f32[3,1,96,128]{3,2,0,1:T(8,128)S(1)} fusion(f32[96,128]{1,0:T(8,128)S(1)} %slice_bitcast_fusion.2, f32[3,1,96,128]{3,2,1,0:T(8,128)} %param.8), kind=kLoop, calls=%fused_computation.56 | loop fusion | flops 36864 | bytes 344064 | tf_op jit(solution)/shard_map/mul | solution.py:70
  1.9 3.1 %collective-permute-start = (f32[6,1,96,128]{3,2,0,1:T(8,128)S(1)}, f32[6,1,96,128]{3,2,0,1:T(8,128)S(1)}, u32[]{:S(2)}, u32[]{:S(2)}) collective-permute-start(f32[6,1,96,128]{3,2,0,1:T(8,128)S(1)} %pad_maximum_fusion), channel_id=1, source_target_pairs={{0,16},{4,20},{8,24},{12,28},{16,0},{20,4},{24,8},{28,12},{1,17},{... | collective-permute-start | bytes 884744 | tf_op jit(solution)/shard_map/ppermute | solution.py:23
  5.1 6.8 %collective-permute-done = f32[6,1,96,128]{3,2,0,1:T(8,128)S(1)} collective-permute-done((f32[6,1,96,128]{3,2,0,1:T(8,128)S(1)}, f32[6,1,96,128]{3,2,0,1:T(8,128)S(1)}, u32[]{:S(2)}, u32[]{:S(2)}) %collective-permute-start) | collective-permute-done | bytes 294944 | tf_op jit(solution)/shard_map/ppermute | solution.py:23
  11.9 0.1 subtract_bitcast_fusion
  12.1 1.8 %collective-permute-start.1 = (f32[2,6,1,96,128]{4,3,1,2,0:T(8,128)S(1)}, f32[2,6,1,96,128]{4,3,1,2,0:T(8,128)S(1)}, u32[]{:S(2)}, u32[]{:S(2)}) collective-permute-start(f32[2,6,1,96,128]{4,3,1,2,0:T(8,128)S(1)} %maximum_select_fusion), channel_id=1, source_target_pairs={{0,8},{4,12},{8,0},{12,4},{16,24},{20,28},{24,16},{28,20},{1,9},{5... | collective-permute-start | bytes 1769480 | tf_op jit(solution)/shard_map/ppermute | solution.py:23
  14.0 12.6 %collective-permute-done.1 = f32[2,6,1,96,128]{4,3,1,2,0:T(8,128)S(1)} collective-permute-done((f32[2,6,1,96,128]{4,3,1,2,0:T(8,128)S(1)}, f32[2,6,1,96,128]{4,3,1,2,0:T(8,128)S(1)}, u32[]{:S(2)}, u32[]{:S(2)}) %collective-permute-start.1) | collective-permute-done | bytes 589856 | tf_op jit(solution)/shard_map/ppermute | solution.py:23
  26.6 0.1 multiply_subtract_fusion.1
  26.7 0.1 maximum_select_fusion.1
  27.0 0.3 fusion.31
  27.3 1.6 %collective-permute-done.2 = f32[2,6,1,96,128]{4,3,1,2,0:T(8,128)S(1)} collective-permute-done((f32[2,6,1,96,128]{4,3,1,2,0:T(8,128)S(1)}, f32[2,6,1,96,128]{4,3,1,2,0:T(8,128)S(1)}, u32[]{:S(2)}, u32[]{:S(2)}) %collective-permute-start.2) | collective-permute-done | bytes 589856 | tf_op jit(solution)/shard_map/ppermute | solution.py:23
  29.0 0.1 maximum_select_fusion.2
  29.2 0.6 fusion.8
  29.9 0.4 convolution_bitcast_fusion
  30.3 0.2 copy.25
  30.5 0.1 fusion.11
  30.6 3.6 %collective-permute-start.3 = (f32[3,1,96,1,64]{2,4,3,0,1:T(8,128)S(1)}, f32[3,1,96,1,64]{2,4,3,0,1:T(8,128)S(1)}, u32[]{:S(2)}, u32[]{:S(2)}) collective-permute-start(f32[3,1,96,1,64]{2,4,3,0,1:T(8,128)S(1)} %get-tuple-element.225), channel_id=1, source_target_pairs={{0,3},{1,0},{2,1},{3,2},{4,7},{5,4},{6,5},{7,6},{8,11},{9,8},{10,9... | collective-permute-start | bytes 221192 | tf_op jit(solution)/shard_map/ppermute | solution.py:17
  34.2 1.0 %collective-permute-start.5 = (f32[3,1,96,1,64]{2,4,3,0,1:T(8,128)S(1)}, f32[3,1,96,1,64]{2,4,3,0,1:T(8,128)S(1)}, u32[]{:S(2)}, u32[]{:S(2)}) collective-permute-start(f32[3,1,96,1,64]{2,4,3,0,1:T(8,128)S(1)} %get-tuple-element.223), channel_id=1, source_target_pairs={{0,1},{1,2},{2,3},{3,0},{4,5},{5,6},{6,7},{7,4},{8,9},{9,10},{10,1... | collective-permute-start | bytes 221192 | tf_op jit(solution)/shard_map/ppermute | solution.py:17
  35.2 16.9 %all_gather.6 = f32[384,96]{1,0:T(8,128)S(1)} all-gather(f32[96,96]{1,0:T(8,128)S(1)} %copy-done.2), channel_id=1, replica_groups=mesh['gx'=8,'gy'=4] {'gy'}, dimensions={0}, use_global_device_ids=true | all-gather | bytes 184320 | tf_op jit(solution)/shard_map/all_gather | solution.py:117
  52.1 13.6 %all_gather.7 = f32[384,96]{1,0:T(8,128)S(1)} all-gather(f32[96,96]{1,0:T(8,128)S(1)} %copy-done.3), channel_id=1, replica_groups=mesh['gx'=8,'gy'=4] {'gy'}, dimensions={0}, use_global_device_ids=true | all-gather | bytes 184320 | tf_op jit(solution)/shard_map/all_gather | solution.py:118
  65.7 0.3 concatenate.35
  66.0 0.1 constant_dynamic-slice_fusion.1
  66.2 0.3 reshape.108
  66.5 1.7 %while.30 = (s32[]{:T(128)}, f32[3,1,96,64]{2,3,0,1:T(8,128)S(1)}, f32[4,3,1,96,64]{3,4,1,2,0:T(8,128)S(1)}, f32[4,3,1,96,64]{3,0,4,1,2:T(4,128)S(1)}, f32[4,96,96]{2,1,0:T(8,128)S(1)}, /*index=5*/s32[]{:T(128)}, s32[]{:T(128)}) while((s32[]{:T(128)}, f32[3,1,96,64]{2,3,0,1:T(8,128)S(1)}, f32[4,3,1,96,64]{3,4,1,2,0:T(8,128)S(1)}, ...), condition=%wide.region_1.2_spmd.clone, body=%wide.region_0.1_spmd.clone.sunk | while | flops 21270532 | bytes 933987 | solution.py:64
  66.5 0.3 fusion.48
  66.8 0.1 constant_dynamic-slice_fusion.3
  66.9 0.3 fusion.48
  67.2 0.1 constant_dynamic-slice_fusion.3
  67.4 0.3 fusion.48
  67.6 0.1 constant_dynamic-slice_fusion.3
  67.8 0.3 fusion.48
  68.1 0.1 constant_dynamic-slice_fusion.3
  68.2 1.3 %while.31 = (s32[]{:T(128)}, f32[3,1,96,64]{2,3,0,1:T(8,128)S(1)}, f32[4,3,1,96,64]{3,4,1,2,0:T(8,128)S(1)}, f32[4,3,1,96,64]{3,4,1,2,0:T(8,128)S(1)}, f32[4,96,...) while((s32[]{:T(128)}, f32[3,1,96,64]{2,3,0,1:T(8,128)S(1)}, ...), condition=%wide.region_3.4_spmd.clone, body=%wide.region_2.3_spmd.clone.sunk | while | flops 21270532 | bytes 786547 | solution.py:65
  68.3 0.2 fusion.51
  68.6 0.3 fusion.51
  68.9 0.2 fusion.51
  69.3 0.3 fusion.51
  69.6 0.3 copy.32
  69.9 0.7 reshape.121
  70.6 0.5 broadcast.112
  71.2 2.6 %reduce = f32[384,3,64]{2,1,0:T(4,128)S(1)} reduce(f32[384,3,1,1,64]{4,3,2,1,0:T(1,128)S(1)} %bitcast.124, f32[]{:T(128)} %broadcast.112), dimensions={2,3}, to_apply=%bitcast.90.reduce_sub_computation | reduce | bytes 589828
  73.7 0.6 reshape.122
  74.3 10.3 %all_to_all.15 = f32[4,1,18432]{2,1,0:T(1,128)S(1)} all-to-all(f32[4,1,18432]{2,1,0:T(1,128)S(1)} %reshape.122), channel_id=1, replica_groups=mesh['gx'=8,'gy'=4] {'gy'}, dimensions={0} | all-to-all | bytes 589824 | tf_op jit(solution)/shard_map/all_to_all | solution.py:131
  84.6 1.5 %reduce.1 = f32[4,18432]{1,0:T(4,128)S(1)} reduce(f32[4,1,18432]{2,1,0:T(1,128)S(1)} %all_to_all.15, f32[]{:T(128)} %broadcast.112), dimensions={1}, to_apply=%all_to_all.11.reduce_sub_computation | reduce | bytes 589828 | tf_op jit(solution)/shard_map/all_to_all | solution.py:131
  86.1 0.7 reshape.123
  86.8 0.8 copy.29
  87.6 0.3 all_to_all.12
  87.9 0.9 copy.31
  (42 shorter events, 0.7 us)
Async XLA Ops:
  0.0 29.9 %copy-start = (f32[96,96]{1,0:T(8,128)S(1)}, f32[96,96]{1,0:T(8,128)}, u32[]{:S(2)}) copy-start(f32[96,96]{1,0:T(8,128)} %param.9) | copy-start | bytes 110596
  0.8 1.0 %copy-start.1 = (f32[3,1,96,128]{3,2,1,0:T(8,128)S(1)}, f32[3,1,96,128]{3,2,1,0:T(8,128)}, u32[]{:S(2)}) copy-start(f32[3,1,96,128]{3,2,1,0:T(8,128)} %param.8) | copy-start | bytes 442372
  1.9 10.1 %collective-permute-start = (f32[6,1,96,128]{3,2,0,1:T(8,128)S(1)}, f32[6,1,96,128]{3,2,0,1:T(8,128)S(1)}, u32[]{:S(2)}, u32[]{:S(2)}) collective-permute-start(f32[6,1,96,128]{3,2,0,1:T(8,128)S(1)} %pad_maximum_fusion), channel_id=1, source_target_pairs={{0,16},{4,20},{8,24},{12,28},{16,0},{20,4},{24,8},{28,12},{1,17},{... | collective-permute-start | bytes 884744 | tf_op jit(solution)/shard_map/ppermute | solution.py:23
  12.1 14.6 %collective-permute-start.1 = (f32[2,6,1,96,128]{4,3,1,2,0:T(8,128)S(1)}, f32[2,6,1,96,128]{4,3,1,2,0:T(8,128)S(1)}, u32[]{:S(2)}, u32[]{:S(2)}) collective-permute-start(f32[2,6,1,96,128]{4,3,1,2,0:T(8,128)S(1)} %maximum_select_fusion), channel_id=1, source_target_pairs={{0,8},{4,12},{8,0},{12,4},{16,24},{20,28},{24,16},{28,20},{1,9},{5... | collective-permute-start | bytes 1769480 | tf_op jit(solution)/shard_map/ppermute | solution.py:23
  26.9 2.1 %collective-permute-start.2 = (f32[2,6,1,96,128]{4,3,1,2,0:T(8,128)S(1)}, f32[2,6,1,96,128]{4,3,1,2,0:T(8,128)S(1)}, u32[]{:S(2)}, u32[]{:S(2)}) collective-permute-start(f32[2,6,1,96,128]{4,3,1,2,0:T(8,128)S(1)} %maximum_select_fusion.1), channel_id=1, source_target_pairs={{0,4},{4,0},{8,12},{12,8},{16,20},{20,16},{24,28},{28,24},{1,5},{5... | collective-permute-start | bytes 1769480 | tf_op jit(solution)/shard_map/ppermute | solution.py:23
  30.6 4.7 %copy-start.2 = (f32[96,96]{1,0:T(8,128)S(1)}, f32[96,96]{1,0:T(8,128)}, u32[]{:S(2)}) copy-start(f32[96,96]{1,0:T(8,128)} %param.10) | copy-start | bytes 110596
  30.6 35.1 %collective-permute-start.3 = (f32[3,1,96,1,64]{2,4,3,0,1:T(8,128)S(1)}, f32[3,1,96,1,64]{2,4,3,0,1:T(8,128)S(1)}, u32[]{:S(2)}, u32[]{:S(2)}) collective-permute-start(f32[3,1,96,1,64]{2,4,3,0,1:T(8,128)S(1)} %get-tuple-element.225), channel_id=1, source_target_pairs={{0,3},{1,0},{2,1},{3,2},{4,7},{5,4},{6,5},{7,6},{8,11},{9,8},{10,9... | collective-permute-start | bytes 221192 | tf_op jit(solution)/shard_map/ppermute | solution.py:17
  34.2 31.5 %collective-permute-start.4 = (f32[3,1,96,1,64]{2,4,3,0,1:T(8,128)S(1)}, f32[3,1,96,1,64]{2,4,3,0,1:T(8,128)S(1)}, u32[]{:S(2)}, u32[]{:S(2)}) collective-permute-start(f32[3,1,96,1,64]{2,4,3,0,1:T(8,128)S(1)} %get-tuple-element.224), channel_id=1, source_target_pairs={{0,2},{1,3},{2,0},{3,1},{4,6},{5,7},{6,4},{7,5},{8,10},{9,11},{10,... | collective-permute-start | bytes 221192 | tf_op jit(solution)/shard_map/ppermute | solution.py:17
  34.2 31.5 %collective-permute-start.5 = (f32[3,1,96,1,64]{2,4,3,0,1:T(8,128)S(1)}, f32[3,1,96,1,64]{2,4,3,0,1:T(8,128)S(1)}, u32[]{:S(2)}, u32[]{:S(2)}) collective-permute-start(f32[3,1,96,1,64]{2,4,3,0,1:T(8,128)S(1)} %get-tuple-element.223), channel_id=1, source_target_pairs={{0,1},{1,2},{2,3},{3,0},{4,5},{5,6},{6,7},{7,4},{8,9},{9,10},{10,1... | collective-permute-start | bytes 221192 | tf_op jit(solution)/shard_map/ppermute | solution.py:17
  35.2 16.9 %copy-start.3 = (f32[96,96]{1,0:T(8,128)S(1)}, f32[96,96]{1,0:T(8,128)}, u32[]{:S(2)}) copy-start(f32[96,96]{1,0:T(8,128)} %param.11) | copy-start | bytes 110596
